TPU v7x, 128 devices: a whole 4x4x4 slice. The times are simulated.
128 devices in a mesh: row: 16 (over x_lo, z, core), col: 8 (over y, x_hi).
Axes of the slice: x: 4 (x_hi: 2, x_lo: 2; x = x_hi * 2 + x_lo), y: 4, z: 4, core: 2. Of those that a mesh axis runs over, the one named last changes fastest.
Arguments:
- new_velocity: float32 [3, 160, 160, 160], P(None, 'row', 'col'), may hold values from -6 to 6
- stored_velocity: float32 [6, 3, 256, 256, 256], P(None, None, 'row', 'col'), may hold values from -6 to 6
- stored_vorticity: float32 [6, 3, 256, 256, 256], P(None, None, 'row', 'col'), may hold values from -6 to 6
Outputs:
- next_velocity: float32 [3, 160, 160, 160], P(None, 'row', 'col')
All inputs are finite; a program needn't handle non-finite values.
Results may differ from a plain program's by a relative error of at most 0.00007.
Values sent between devices are 32-bit elements; how exact they have to be, the bound alone decides.
A program may use at most 128 MiB of HBM per device.

v0:
```python
import jax
import jax.numpy as jnp
import numpy as np
from jax import lax
from jax.experimental import pallas as pl
from jax.experimental.pallas import tpu as pltpu
from jax.sharding import PartitionSpec as P

N = 256
MODES = 160
ORDERS = 6
KMAX = 79
ROWS, COLS = 16, 8
KY, KZ = MODES // ROWS, MODES // COLS
XL, YL = N // ROWS, N // COLS
CHUNKS = 4
XC = XL // CHUNKS
XP = XC // 2
OFFSETS = (0, 20, 40, 64, 84, 104)
MESH = pl.DeviceIdType.MESH
bf16, f32 = jnp.bfloat16, jnp.float32


def basis():
    p = np.arange(N)[:, None]
    m = np.arange(MODES)[None, :]
    k = m // 2
    angle = 2.0 * np.pi / N * (p * k % N)
    table = np.where(m % 2 == 0, np.cos(angle), np.sin(angle)) * np.sqrt(np.where(m < 2, 1.0, 2.0) / N)
    table[:, 1] = 0.0
    return table


def halves(table):
    high = np.asarray(table, jnp.bfloat16)
    low = np.asarray(table - high.astype(np.float64), jnp.bfloat16)
    return high, low


def tables():
    s = basis()
    sx = np.zeros((N, 256))
    sx[:, :MODES] = s
    order = np.arange(MODES).reshape(ROWS, KY).T.reshape(-1)
    sy_h, sy_l = halves(s[:, order])
    sy = np.concatenate([sy_h, sy_h, sy_l, np.zeros((N, 32), jnp.bfloat16)], axis=1)
    sz = np.zeros((256, N))
    sz[:120] = s[:, :120].T
    sz[128:168] = s[:, 120:].T
    ya = np.concatenate([sy_h.T, sy_h.T, sy_l.T], axis=1)
    points = np.arange(N).reshape(ROWS, XL // 2, 2).transpose(2, 0, 1).reshape(-1)
    xa = np.zeros((N, 256))
    xa[:, :MODES] = s[points]
    return (*halves(sx), sy, *halves(sz), *halves(sz.T), ya, *halves(xa))


def split(x):
    high = x.astype(bf16)
    return high, (x - high.astype(f32)).astype(bf16)


def dot(a, b):
    return jnp.dot(a, b, preferred_element_type=f32)


def dot_nt(a, b):
    return lax.dot_general(a, b, (((1,), (1,)), ((), ())), preferred_element_type=f32)


def dot3(x, table_h, table_l):
    high, low = split(x)
    return dot(high, table_h[...]) + (dot(low, table_h[...]) + dot(high, table_l[...]))


def roll(x, shift, axis):
    shift %= x.shape[axis]
    return x if shift == 0 else pltpu.roll(x, shift, axis)


def pair_swap(x, axis):
    even = lax.broadcasted_iota(jnp.int32, x.shape, axis) % 2 == 0
    return jnp.where(even, roll(x, -1, axis), -roll(x, 1, axis))


def kernel(
    a_ref, vel_hbm, vort_hbm, sxh, sxl, sy, szh, szl, zah, zal, ya, xah, xal,
    out_ref,
    a_s, f_s, vel, vort, part, send1, recv1, send2, recv2, send3, recv3, send4, recv4, fin,
    hbm_sem, s1s, s1r, s2s, s2r, s3s, s3r, s4s, s4r, own,
):
    r, c = lax.axis_index("row"), lax.axis_index("col")

    def row_peer(i):
        return lax.rem(r + i, ROWS)

    def col_peer(i):
        return lax.rem(c + i, COLS)

    barrier = pltpu.get_barrier_semaphore()
    for i in range(1, ROWS):
        pl.semaphore_signal(barrier, 1, device_id=(row_peer(i), c), device_id_type=MESH)
    for i in range(1, COLS):
        pl.semaphore_signal(barrier, 1, device_id=(r, col_peer(i)), device_id_type=MESH)

    def stored(o):
        return (
            pltpu.make_async_copy(vel_hbm.at[o], vel.at[o], hbm_sem.at[0, o]),
            pltpu.make_async_copy(vort_hbm.at[o], vort.at[o], hbm_sem.at[1, o]),
        )

    for o in (1, 5, 2, 4, 3, 0):
        for copy in stored(o):
            copy.start()

    def ds(start, size, unit):
        return pl.ds(pl.multiple_of(start, unit), size)

    def copy1(h, i):
        there = row_peer(i)
        return pltpu.make_async_remote_copy(
            send1.at[:, ds(there * XL + 8 * h, 8, 8), :],
            recv1.at[:, ds(r * XL + 8 * h, 8, 8), :],
            s1s.at[h, i], s1r.at[h, i], device_id=(there, c), device_id_type=MESH,
        )

    def copy2(g, i):
        there = col_peer(i)
        return pltpu.make_async_remote_copy(
            send2.at[pl.ds(g * XC, XC), ds(there * YL, YL, 8), :],
            recv2.at[c, pl.ds(g * XC, XC)],
            s2s.at[g, i], s2r.at[g, i], device_id=(r, there), device_id_type=MESH,
        )

    def copy3(g, i):
        there = col_peer(i)
        return pltpu.make_async_remote_copy(
            send3.at[there, pl.ds(g * XP, XP)],
            recv3.at[pl.ds(g * XP, XP), ds(c * YL, YL, 8), :],
            s3s.at[g, i], s3r.at[g, i], device_id=(r, there), device_id_type=MESH,
        )

    def copy4(i):
        there = row_peer(i)
        return pltpu.make_async_remote_copy(
            send4.at[:, ds(there * 8, 8, 8), :],
            recv4.at[:, ds(r * 8, 8, 8), :],
            s4s.at[i], s4r.at[i], device_id=(there, c), device_id_type=MESH,
        )

    own1 = pltpu.make_async_copy(send1.at[:, ds(r * XL, XL, 8), :], recv1.at[:, ds(r * XL, XL, 8), :], own.at[0])
    own4 = pltpu.make_async_copy(send4.at[:, ds(r * 8, 8, 8), :], recv4.at[:, ds(r * 8, 8, 8), :], own.at[1])

    def own2(g):
        return pltpu.make_async_copy(
            send2.at[pl.ds(g * XC, XC), ds(c * YL, YL, 8), :], recv2.at[c, pl.ds(g * XC, XC)], own.at[2 + g]
        )

    def own3(g):
        return pltpu.make_async_copy(
            send3.at[c, pl.ds(g * XP, XP)], recv3.at[pl.ds(g * XP, XP), ds(c * YL, YL, 8), :], own.at[2 + CHUNKS + g]
        )

    lane = lax.broadcasted_iota(jnp.int32, (24, 256), 1)
    sub = lax.broadcasted_iota(jnp.int32, (24, 256), 0)
    wave_x = (lane // 2).astype(f32) / KMAX
    wave_z = (sub // 2 + c * (KZ // 2)).astype(f32) / KMAX

    def wave_y(pair):
        return (jnp.zeros((24, 256), jnp.int32) + (r * (KY // 2) + pair)).astype(f32) / KMAX

    def diff_x(v):
        return wave_x * pair_swap(v, 1)

    def diff_z(v):
        return wave_z * pair_swap(v, 0)

    a_s[...] = jnp.zeros_like(a_s)
    f_s[...] = jnp.zeros_like(f_s)

    def fields(pair, carry):
        wy = wave_y(pair)
        for k in range(2):
            for i in range(3):
                a_s[k, i, 0:KZ, 0:MODES] = a_ref[i, 2 * pair + k]
        for k in range(2):
            v = [a_s[k, i] for i in range(3)]
            wy_k = wy if k == 0 else -wy
            dy = [wy_k * a_s[1 - k, i] for i in range(3)]
            v += [dy[2] - diff_z(v[1]), diff_z(v[0]) - diff_x(v[2]), diff_x(v[1]) - dy[0]]
            for i in range(6):
                f_s[128 * k + KZ * i : 128 * k + KZ * (i + 1), :] = v[i][0:KZ]
        high, low = split(f_s[...])
        o = dot_nt(sxh[...], high) + (dot_nt(sxh[...], low) + dot_nt(sxl[...], high))
        send1[2 * pair] = o[:, :128]
        send1[2 * pair + 1] = o[:, 128:]
        return carry

    lax.fori_loop(0, KY // 2, fields, 0)

    own1.start()
    pl.semaphore_wait(barrier, ROWS + COLS - 2)
    for h in range(2):
        for i in range(1, ROWS):
            copy1(h, i).start()

    for o in (1, 5, 2, 4, 3):
        for copy in stored(o):
            copy.wait()

    def old_terms(x, carry):
        acc = None
        for o in range(1, ORDERS):
            u = [vel[o, i, x] for i in range(3)]
            w = [vort[ORDERS - o, i, x] for i in range(3)]
            term = [u[1] * w[2] - u[2] * w[1], u[2] * w[0] - u[0] * w[2], u[0] * w[1] - u[1] * w[0]]
            acc = term if acc is None else [p + q for p, q in zip(acc, term)]
        for i in range(3):
            part[i, x] = acc[i]
        return carry

    lax.fori_loop(0, XL, old_terms, 0)
    for copy in stored(0):
        copy.wait()

    def synth_y(xp, carry):
        t = []
        for k in range(2):
            rows = pl.ds(2 * xp + k, ROWS, stride=XL)
            t.append(jnp.concatenate([recv1[m, rows, :] for m in range(KY)], axis=0))
        high, low = split(jnp.concatenate(t, axis=1))
        rhs = jnp.concatenate([high, low, high, jnp.zeros((32, 256), bf16)], axis=0)
        o = dot(sy[...], rhs)
        send2[2 * xp] = o[:, :128]
        send2[2 * xp + 1] = o[:, 128:]
        return carry

    own1.wait()
    for h in range(2):
        for i in range(1, ROWS):
            copy1(h, i).wait_recv()
        for g in range(h * CHUNKS // 2, (h + 1) * CHUNKS // 2):
            lax.fori_loop(g * XP, (g + 1) * XP, synth_y, 0)
            own2(g).start()
            for i in range(1, COLS):
                copy2(g, i).start()

    lane_y = lax.broadcasted_iota(jnp.int32, (YL, 128), 1)

    def place(first):
        q = lane_y - first
        return jnp.where(q < 0, q + 128, q)

    def middle(xp, carry):
        sums = []
        for k in range(2):
            x = 2 * xp + k
            blocks = [roll(recv2[m, x], KZ * (m % 6), 1) for m in range(COLS)]
            tile1, tile2 = [], []
            for i in range(6):
                q = place(KZ * i)
                t = blocks[0]
                for m in range(1, 6):
                    t = jnp.where(q >= KZ * m, blocks[m], t)
                tile1.append(roll(t, -KZ * i, 1))
                tile2.append(roll(jnp.where(q >= KZ, blocks[7], blocks[6]), -KZ * i, 1))
            modes = jnp.concatenate([jnp.concatenate(tile1, axis=0), jnp.concatenate(tile2, axis=0)], axis=1)
            new = dot3(modes, szh, szl)
            u = [new[YL * i : YL * (i + 1)] for i in range(3)]
            w = [new[YL * i : YL * (i + 1)] for i in range(3, 6)]
            v0 = [vel[0, i, x] for i in range(3)]
            w0 = [vort[0, i, x] for i in range(3)]
            for i in range(3):
                a, b = (i + 1) % 3, (i + 2) % 3
                sums.append(part[i, x] + ((u[a] * w0[b] - u[b] * w0[a]) + (v0[a] * w[b] - v0[b] * w[a])))
        o = dot3(jnp.concatenate(sums, axis=0), zah, zal)
        out = [o[YL * j : YL * (j + 1)] for j in range(6)]
        for half in range(2):
            rolled = [roll(out[j][:, 128 * half : 128 * half + 128], OFFSETS[j], 1) for j in range(6)]
            for m in range(6 if half == 0 else 2):
                q = place(KZ * m)
                t = rolled[0]
                for j in range(1, 6):
                    t = jnp.where(q >= OFFSETS[j], rolled[j], t)
                send3[6 * half + m, xp] = roll(t, -KZ * m, 1)
        return carry

    for g in range(CHUNKS):
        own2(g).wait()
        for i in range(1, COLS):
            copy2(g, i).wait_recv()
        lax.fori_loop(g * XP, (g + 1) * XP, middle, 0)
        own3(g).start()
        for i in range(1, COLS):
            copy3(g, i).start()

    def analyze_y(xq, carry):
        high, low = split(jnp.concatenate([recv3[2 * xq], recv3[2 * xq + 1]], axis=1))
        o = dot(ya[...], jnp.concatenate([high, low, high], axis=0))
        for k in range(2):
            for m in range(KY):
                send4[m, pl.ds(2 * xq + k, ROWS, stride=8), :] = o[ROWS * m : ROWS * (m + 1), 128 * k : 128 * k + 128]
        return carry

    for g in range(CHUNKS):
        own3(g).wait()
        for i in range(1, COLS):
            copy3(g, i).wait_recv()
        lax.fori_loop(g * XP // 2, (g + 1) * XP // 2, analyze_y, 0)
    own4.start()
    for i in range(1, ROWS):
        copy4(i).start()
    own4.wait()
    for i in range(1, ROWS):
        copy4(i).wait_recv()

    def finish(pair, carry):
        rows = []
        for k in range(2):
            t = recv4[2 * pair + k].T
            rows.append(jnp.concatenate([t[0:64], t[64:128]], axis=1))
        fin[...] = dot3(jnp.concatenate(rows, axis=0), xah, xal)
        s = [[fin[64 * k + KZ * i : 64 * k + KZ * i + 24, :] for i in range(3)] for k in range(2)]
        wy = wave_y(pair)
        square = wave_y(pair) ** 2 + wave_z**2 + wave_x**2
        some = square > 0
        safe = jnp.where(some, square, 1.0)
        potential = []
        for k in range(2):
            wy_k = wy if k == 0 else -wy
            divergence = diff_x(s[k][0]) + wy_k * s[1 - k][1] + diff_z(s[k][2])
            potential.append(jnp.where(some, divergence / safe, 0.0))
        for k in range(2):
            wy_k = wy if k == 0 else -wy
            slopes = (diff_x(potential[k]), wy_k * potential[1 - k], diff_z(potential[k]))
            for i in range(3):
                out_ref[i, 2 * pair + k] = ((s[k][i] + slopes[i]) / (ORDERS + 1))[0:KZ, 0:MODES]
        return carry

    lax.fori_loop(0, KY // 2, finish, 0)

    for i in range(1, ROWS):
        copy1(0, i).wait_send()
        copy1(1, i).wait_send()
        copy4(i).wait_send()
    for g in range(CHUNKS):
        for i in range(1, COLS):
            copy2(g, i).wait_send()
            copy3(g, i).wait_send()


def shards(new_velocity, stored_velocity, stored_vorticity):
    consts = tables()
    vmem = pl.BlockSpec(memory_space=pltpu.VMEM)
    hbm = pl.BlockSpec(memory_space=pl.ANY)
    dma = pltpu.SemaphoreType.DMA
    return pl.pallas_call(
        kernel,
        out_shape=jax.ShapeDtypeStruct((3, KY, KZ, MODES), f32),
        in_specs=[vmem, hbm, hbm] + [vmem] * len(consts),
        out_specs=vmem,
        scratch_shapes=[
            pltpu.VMEM((2, 3, 24, 256), f32),
            pltpu.VMEM((256, 256), f32),
            pltpu.VMEM((ORDERS, 3, XL, YL, N), f32),
            pltpu.VMEM((ORDERS, 3, XL, YL, N), f32),
            pltpu.VMEM((3, XL, YL, N), f32),
            pltpu.VMEM((KY, N, 128), f32),
            pltpu.VMEM((KY, N, 128), f32),
            pltpu.VMEM((XL, N, 128), f32),
            pltpu.VMEM((COLS, XL, YL, 128), f32),
            pltpu.VMEM((COLS, XL // 2, YL, 128), f32),
            pltpu.VMEM((XL // 2, N, 128), f32),
            pltpu.VMEM((KY, 128, 128), f32),
            pltpu.VMEM((KY, 128, 128), f32),
            pltpu.VMEM((128, 256), f32),
            dma((2, ORDERS)),
            dma((2, ROWS)),
            dma((2, ROWS)),
            dma((CHUNKS, COLS)),
            dma((CHUNKS, COLS)),
            dma((CHUNKS, COLS)),
            dma((CHUNKS, COLS)),
            dma((ROWS,)),
            dma((ROWS,)),
            dma((2 + 2 * CHUNKS,)),
        ],
        compiler_params=pltpu.CompilerParams(
            collective_id=0, has_side_effects=True, vmem_limit_bytes=60 * 2**20
        ),
        name="euler_order",
    )(new_velocity, stored_velocity, stored_vorticity, *map(jnp.asarray, consts))


def solution(mesh):
    return jax.shard_map(
        shards,
        mesh=mesh,
        in_specs=(
            P(None, "row", "col", None),
            P(None, None, "row", "col", None),
            P(None, None, "row", "col", None),
        ),
        out_specs=P(None, "row", "col", None),
        check_vma=False,
    )
```

profile of v0, /device:TPU:1, one launch (start us, length us, event | category | flops | bytes accessed | tf_op | source)
XLA Modules:
  0.0 76.4 jit_solution(912478956288477408)
XLA Ops:
  0.0 74.3 %euler_order.1 = f32[3,10,20,160]{3,2,1,0:T(8,128)} custom-call(f32[3,10,20,160]{3,2,1,0:T(8,128)} %a_ref.1, f32[6,3,16,32,256]{4,3,2,1,0:T(8,128)} %vel_hbm.1, f32[6,3,16,32,256]{4,3,2,1,0:T(8,128)} %vort_hbm.1, bf16[256,256]{1,0:T(8,128)(2,1)} %constant.20.clone.sxh, bf16[256,256]{1,0:T(8,128)(2,1)} %constant.21.clone.sxl, ...), custom_call_target="tpu_custom_call" | custom-call | tf_op jit(solution)/shard_map/euler_order/pallas_call | solution.py:356
  74.4 2.0 %copy.15 = f32[3,10,20,160]{3,2,1,0:T(8,128)} copy(f32[3,10,20,160]{3,2,1,0:T(8,128)} %euler_order.1) | data formatting | bytes 768000
where the time goes:
time: 76.6 us; the launch traced here: 76.4 us
  Pallas kernels  74.3 us (97%)
  local copies, waits for them, and re-layouts  2.03 us (3%)
    pallas_call x1, Pallas kernels, shards(): pl.pallas_call(kernel, out_shape=jax.ShapeDtypeStruct((3, KY, KZ, MODES),...  74.3 us
    unnamed x1, local copies, waits for them, and re-layouts  2.03 us

commit v1 on v0

--- a/solution.py
+++ b/solution.py
@@ -17,6 +17,7 @@
 XC = XL // CHUNKS
 XP = XC // 2
 OFFSETS = (0, 20, 40, 64, 84, 104)
+TABLES = 8
 MESH = pl.DeviceIdType.MESH
 bf16, f32 = jnp.bfloat16, jnp.float32
 
@@ -48,9 +49,11 @@
     sz[:120] = s[:, :120].T
     sz[128:168] = s[:, 120:].T
     ya = np.concatenate([sy_h.T, sy_h.T, sy_l.T], axis=1)
-    points = np.arange(N).reshape(ROWS, XL // 2, 2).transpose(2, 0, 1).reshape(-1)
-    xa = np.zeros((N, 256))
-    xa[:, :MODES] = s[points]
+    points = np.arange(N).reshape(ROWS, 2, 4, 2).transpose(1, 3, 0, 2)
+    xa = np.zeros((2, 2, ROWS, 2, 4, 2, 256))
+    for k in range(2):
+        xa[:, :, :, k, :, k, :MODES] = s[points]
+    xa = xa.reshape(512, 512)
     return (*halves(sx), sy, *halves(sz), *halves(sz.T), ya, *halves(xa))
 
 
@@ -83,11 +86,14 @@
 
 
 def kernel(
-    a_ref, vel_hbm, vort_hbm, sxh, sxl, sy, szh, szl, zah, zal, ya, xah, xal,
-    out_ref,
+    a_ref, vel_hbm, vort_hbm, sxh, sxl, *rest,
+):
+    tables_hbm, (out_ref, *tables_vmem), rest = rest[:TABLES], rest[TABLES : 2 * TABLES + 1], rest[2 * TABLES + 1 :]
+    sy, szh, szl, zah, zal, ya, xah, xal = tables_vmem
+    (
     a_s, f_s, vel, vort, part, send1, recv1, send2, recv2, send3, recv3, send4, recv4, fin,
-    hbm_sem, s1s, s1r, s2s, s2r, s3s, s3r, s4s, s4r, own,
-):
+    hbm_sem, table_sem, s1s, s1r, s2s, s2r, s3s, s3r, s4s, s4r, own,
+    ) = rest
     r, c = lax.axis_index("row"), lax.axis_index("col")
 
     def row_peer(i):
@@ -108,6 +114,11 @@
             pltpu.make_async_copy(vort_hbm.at[o], vort.at[o], hbm_sem.at[1, o]),
         )
 
+    def table(i):
+        return pltpu.make_async_copy(tables_hbm[i], tables_vmem[i], table_sem.at[i])
+
+    for i in range(TABLES):
+        table(i).start()
     for o in (1, 5, 2, 4, 3, 0):
         for copy in stored(o):
             copy.start()
@@ -139,25 +150,29 @@
             s3s.at[g, i], s3r.at[g, i], device_id=(r, there), device_id_type=MESH,
         )
 
-    def copy4(i):
+    def copy4(h, i):
         there = row_peer(i)
         return pltpu.make_async_remote_copy(
-            send4.at[:, ds(there * 8, 8, 8), :],
-            recv4.at[:, ds(r * 8, 8, 8), :],
-            s4s.at[i], s4r.at[i], device_id=(there, c), device_id_type=MESH,
+            send4.at[h, :, ds(there * 8, 8, 8), :],
+            recv4.at[h, :, ds(r * 8, 8, 8), :],
+            s4s.at[h, i], s4r.at[h, i], device_id=(there, c), device_id_type=MESH,
         )
 
     own1 = pltpu.make_async_copy(send1.at[:, ds(r * XL, XL, 8), :], recv1.at[:, ds(r * XL, XL, 8), :], own.at[0])
-    own4 = pltpu.make_async_copy(send4.at[:, ds(r * 8, 8, 8), :], recv4.at[:, ds(r * 8, 8, 8), :], own.at[1])
+
+    def own4(h):
+        return pltpu.make_async_copy(
+            send4.at[h, :, ds(r * 8, 8, 8), :], recv4.at[h, :, ds(r * 8, 8, 8), :], own.at[1 + h]
+        )
 
     def own2(g):
         return pltpu.make_async_copy(
-            send2.at[pl.ds(g * XC, XC), ds(c * YL, YL, 8), :], recv2.at[c, pl.ds(g * XC, XC)], own.at[2 + g]
+            send2.at[pl.ds(g * XC, XC), ds(c * YL, YL, 8), :], recv2.at[c, pl.ds(g * XC, XC)], own.at[3 + g]
         )
 
     def own3(g):
         return pltpu.make_async_copy(
-            send3.at[c, pl.ds(g * XP, XP)], recv3.at[pl.ds(g * XP, XP), ds(c * YL, YL, 8), :], own.at[2 + CHUNKS + g]
+            send3.at[c, pl.ds(g * XP, XP)], recv3.at[pl.ds(g * XP, XP), ds(c * YL, YL, 8), :], own.at[3 + CHUNKS + g]
         )
 
     lane = lax.broadcasted_iota(jnp.int32, (24, 256), 1)
@@ -203,6 +218,8 @@
         for i in range(1, ROWS):
             copy1(h, i).start()
 
+    for i in range(TABLES):
+        table(i).wait()
     for o in (1, 5, 2, 4, 3):
         for copy in stored(o):
             copy.wait()
@@ -293,35 +310,49 @@
         for i in range(1, COLS):
             copy3(g, i).start()
 
-    def analyze_y(xq, carry):
+    def analyze_y(h, xq):
         high, low = split(jnp.concatenate([recv3[2 * xq], recv3[2 * xq + 1]], axis=1))
         o = dot(ya[...], jnp.concatenate([high, low, high], axis=0))
         for k in range(2):
             for m in range(KY):
-                send4[m, pl.ds(2 * xq + k, ROWS, stride=8), :] = o[ROWS * m : ROWS * (m + 1), 128 * k : 128 * k + 128]
-        return carry
-
-    for g in range(CHUNKS):
-        own3(g).wait()
-        for i in range(1, COLS):
-            copy3(g, i).wait_recv()
-        lax.fori_loop(g * XP // 2, (g + 1) * XP // 2, analyze_y, 0)
-    own4.start()
-    for i in range(1, ROWS):
-        copy4(i).start()
-    own4.wait()
-    for i in range(1, ROWS):
-        copy4(i).wait_recv()
+                rows = pl.ds(4 * (m % 2) + 2 * xq - 4 * h + k, ROWS, stride=8)
+                send4[h, m // 2, rows, :] = o[ROWS * m : ROWS * (m + 1), 128 * k : 128 * k + 128]
+
+    def analyze_x(h):
+        rows = []
+        for m in range(KY // 2):
+            t = recv4[h, m].T
+            rows.append(jnp.concatenate([t[0:64], t[64:128]], axis=1))
+        high, low = split(jnp.concatenate(rows, axis=0))
+        part_h, part_l = xah[256 * h : 256 * h + 256, :], xal[256 * h : 256 * h + 256, :]
+        return dot(high, part_h) + (dot(low, part_h) + dot(high, part_l))
+
+    for h in range(2):
+        for g in range(h * CHUNKS // 2, (h + 1) * CHUNKS // 2):
+            own3(g).wait()
+            for i in range(1, COLS):
+                copy3(g, i).wait_recv()
+            for q in range(g * XP // 2, (g + 1) * XP // 2):
+                analyze_y(h, q)
+        own4(h).start()
+        for i in range(1, ROWS):
+            copy4(h, i).start()
+    for h in range(2):
+        own4(h).wait()
+        for i in range(1, ROWS):
+            copy4(h, i).wait_recv()
+        if h == 0:
+            fin[...] = analyze_x(0)
+        else:
+            fin[...] += analyze_x(1)
 
     def finish(pair, carry):
-        rows = []
-        for k in range(2):
-            t = recv4[2 * pair + k].T
-            rows.append(jnp.concatenate([t[0:64], t[64:128]], axis=1))
-        fin[...] = dot3(jnp.concatenate(rows, axis=0), xah, xal)
-        s = [[fin[64 * k + KZ * i : 64 * k + KZ * i + 24, :] for i in range(3)] for k in range(2)]
+        first = 64 * pair
+        s = [
+            [fin[first + KZ * i : first + KZ * i + 24, 256 * k : 256 * k + 256] for i in range(3)] for k in range(2)
+        ]
         wy = wave_y(pair)
-        square = wave_y(pair) ** 2 + wave_z**2 + wave_x**2
+        square = wy**2 + wave_z**2 + wave_x**2
         some = square > 0
         safe = jnp.where(some, square, 1.0)
         potential = []
@@ -333,15 +364,16 @@
             wy_k = wy if k == 0 else -wy
             slopes = (diff_x(potential[k]), wy_k * potential[1 - k], diff_z(potential[k]))
             for i in range(3):
-                out_ref[i, 2 * pair + k] = ((s[k][i] + slopes[i]) / (ORDERS + 1))[0:KZ, 0:MODES]
+                out_ref[i, 2 * pair + k] = (s[k][i] + slopes[i])[0:KZ, 0:MODES]
         return carry
 
-    lax.fori_loop(0, KY // 2, finish, 0)
-
-    for i in range(1, ROWS):
-        copy1(0, i).wait_send()
-        copy1(1, i).wait_send()
-        copy4(i).wait_send()
+    for pair in range(KY // 2):
+        finish(pair, 0)
+
+    for h in range(2):
+        for i in range(1, ROWS):
+            copy1(h, i).wait_send()
+            copy4(h, i).wait_send()
     for g in range(CHUNKS):
         for i in range(1, COLS):
             copy2(g, i).wait_send()
@@ -353,12 +385,13 @@
     vmem = pl.BlockSpec(memory_space=pltpu.VMEM)
     hbm = pl.BlockSpec(memory_space=pl.ANY)
     dma = pltpu.SemaphoreType.DMA
-    return pl.pallas_call(
+    sums = pl.pallas_call(
         kernel,
         out_shape=jax.ShapeDtypeStruct((3, KY, KZ, MODES), f32),
-        in_specs=[vmem, hbm, hbm] + [vmem] * len(consts),
+        in_specs=[vmem, hbm, hbm, vmem, vmem] + [hbm] * TABLES,
         out_specs=vmem,
         scratch_shapes=[
+            *(pltpu.VMEM(t.shape, bf16) for t in consts[2:]),
             pltpu.VMEM((2, 3, 24, 256), f32),
             pltpu.VMEM((256, 256), f32),
             pltpu.VMEM((ORDERS, 3, XL, YL, N), f32),
@@ -370,25 +403,27 @@
             pltpu.VMEM((COLS, XL, YL, 128), f32),
             pltpu.VMEM((COLS, XL // 2, YL, 128), f32),
             pltpu.VMEM((XL // 2, N, 128), f32),
-            pltpu.VMEM((KY, 128, 128), f32),
-            pltpu.VMEM((KY, 128, 128), f32),
-            pltpu.VMEM((128, 256), f32),
+            pltpu.VMEM((2, KY // 2, 128, 128), f32),
+            pltpu.VMEM((2, KY // 2, 128, 128), f32),
+            pltpu.VMEM((KY // 2 * 64, 512), f32),
             dma((2, ORDERS)),
+            dma((TABLES,)),
             dma((2, ROWS)),
             dma((2, ROWS)),
             dma((CHUNKS, COLS)),
             dma((CHUNKS, COLS)),
             dma((CHUNKS, COLS)),
             dma((CHUNKS, COLS)),
-            dma((ROWS,)),
-            dma((ROWS,)),
-            dma((2 + 2 * CHUNKS,)),
+            dma((2, ROWS)),
+            dma((2, ROWS)),
+            dma((3 + 2 * CHUNKS,)),
         ],
         compiler_params=pltpu.CompilerParams(
             collective_id=0, has_side_effects=True, vmem_limit_bytes=60 * 2**20
         ),
         name="euler_order",
     )(new_velocity, stored_velocity, stored_vorticity, *map(jnp.asarray, consts))
+    return sums / (ORDERS + 1)
 
 
 def solution(mesh):

time: 76.6 us -> 72.5 us (0.946)
  Pallas kernels: 74.3 us -> 70.3 us
  other arithmetic: 0 us -> 2.05 us
  local copies, waits for them, and re-layouts: 2.03 us -> 0 us
    pallas_call x1, Pallas kernels: 74.3 us -> 70.3 us  [shards(): pl.pallas_call(kernel, out_shape=jax.ShapeDtypeStruct((3, KY, KZ, MODES),...]
    div x0 -> x1, other arithmetic: none -> 2.05 us  [shards(): return sums / (ORDERS + 1)]
    unnamed x1 -> x0, local copies, waits for them, and re-layouts: 2.03 us -> none
where the time goes in v1:
time: 72.5 us; the launch traced here: 72.3 us
  Pallas kernels  70.3 us (97%)
  other arithmetic  2.05 us (3%)
    pallas_call x1, Pallas kernels, shards(): pl.pallas_call(kernel, out_shape=jax.ShapeDtypeStruct((3, KY, KZ, MODES),...  70.3 us
    div x1, other arithmetic, shards(): return sums / (ORDERS + 1)  2.05 us

profile of v1, /device:TPU:1, one launch (start us, length us, event | category | flops | bytes accessed | tf_op | source)
XLA Modules:
  0.0 72.3 jit_solution(13774615040521801807)
XLA Ops:
  0.0 70.3 %euler_order.1 = f32[3,10,20,160]{3,2,1,0:T(8,128)} custom-call(f32[3,10,20,160]{3,2,1,0:T(8,128)} %a_ref.1, f32[6,3,16,32,256]{4,3,2,1,0:T(8,128)} %vel_hbm.1, f32[6,3,16,32,256]{4,3,2,1,0:T(8,128)} %vort_hbm.1, bf16[256,256]{1,0:T(8,128)(2,1)} %constant.23.clone.sxh, bf16[256,256]{1,0:T(8,128)(2,1)} %constant.24.clone.sxl, ...), custom_call_target="tpu_custom_call" | custom-call | tf_op jit(solution)/shard_map/euler_order/pallas_call | solution.py:388
  70.3 2.0 %broadcast_multiply_fusion = f32[3,10,20,160]{3,2,1,0:T(8,128)} fusion(f32[3,10,20,160]{3,2,1,0:T(8,128)} %euler_order.1), kind=kLoop, calls=%fused_computation | loop fusion | flops 96000 | bytes 768000 | tf_op jit(solution)/shard_map/div | solution.py:426

commit v2 on v1

--- a/solution.py
+++ b/solution.py
@@ -17,6 +17,7 @@
 XC = XL // CHUNKS
 XP = XC // 2
 OFFSETS = (0, 20, 40, 64, 84, 104)
+TILES = 8
 TABLES = 8
 MESH = pl.DeviceIdType.MESH
 bf16, f32 = jnp.bfloat16, jnp.float32
@@ -191,26 +192,20 @@
 
     a_s[...] = jnp.zeros_like(a_s)
     f_s[...] = jnp.zeros_like(f_s)
-
-    def fields(pair, carry):
-        wy = wave_y(pair)
-        for k in range(2):
-            for i in range(3):
-                a_s[k, i, 0:KZ, 0:MODES] = a_ref[i, 2 * pair + k]
-        for k in range(2):
-            v = [a_s[k, i] for i in range(3)]
-            wy_k = wy if k == 0 else -wy
-            dy = [wy_k * a_s[1 - k, i] for i in range(3)]
-            v += [dy[2] - diff_z(v[1]), diff_z(v[0]) - diff_x(v[2]), diff_x(v[1]) - dy[0]]
-            for i in range(6):
-                f_s[128 * k + KZ * i : 128 * k + KZ * (i + 1), :] = v[i][0:KZ]
-        high, low = split(f_s[...])
+    for m in range(KY):
+        for i in range(3):
+            a_s[i, 0:KZ, 0:MODES] = a_ref[i, m]
+        v = [a_s[i] for i in range(3)]
+        v += [diff_x(v[2]), diff_x(v[1])]
+        for i in range(5):
+            first = KZ * (5 * m + i)
+            f_s[first : first + KZ, :] = v[i][0:KZ]
+
+    for t in range(TILES // 2):
+        high, low = split(f_s[256 * t : 256 * t + 256, :])
         o = dot_nt(sxh[...], high) + (dot_nt(sxh[...], low) + dot_nt(sxl[...], high))
-        send1[2 * pair] = o[:, :128]
-        send1[2 * pair + 1] = o[:, 128:]
-        return carry
-
-    lax.fori_loop(0, KY // 2, fields, 0)
+        send1[2 * t] = o[:, :128]
+        send1[2 * t + 1] = o[:, 128:]
 
     own1.start()
     pl.semaphore_wait(barrier, ROWS + COLS - 2)
@@ -239,11 +234,39 @@
     for copy in stored(0):
         copy.wait()
 
+    lane_r = lax.broadcasted_iota(jnp.int32, (ROWS, 128), 1)
+    sub_r = lax.broadcasted_iota(jnp.int32, (ROWS, 128), 0)
+    slope_z = (lane_r % KZ // 2 + c * (KZ // 2)).astype(f32) / KMAX
+
     def synth_y(xp, carry):
         t = []
         for k in range(2):
             rows = pl.ds(2 * xp + k, ROWS, stride=XL)
-            t.append(jnp.concatenate([recv1[m, rows, :] for m in range(KY)], axis=0))
+            tiles = [recv1[m, rows, :] for m in range(TILES)]
+            sent = []
+            for m in range(KY):
+                tile, first = divmod(5 * KZ * m, 128)
+                block = roll(tiles[tile], -first, 1)
+                if first + 5 * KZ > 128:
+                    block = jnp.where(lane_r < 128 - first, block, roll(tiles[tile + 1], -first, 1))
+                sent.append(block)
+            modes = []
+            for m in range(KY):
+                slope_y = (sub_r * (KY // 2) + m // 2).astype(f32) / KMAX
+                dy = slope_y * (-sent[m - 1] if m % 2 else sent[m + 1])
+                dz = slope_z * pair_swap(sent[m], 1)
+                x_terms = roll(sent[m], KZ, 1)
+                curl_x = roll(dy, KZ, 1) - roll(dz, 2 * KZ, 1)
+                curl_y = roll(dz, 4 * KZ, 1) - x_terms
+                curl_z = x_terms - roll(dy, 5 * KZ, 1)
+                modes.append(
+                    jnp.where(
+                        lane_r < 3 * KZ,
+                        sent[m],
+                        jnp.where(lane_r < 4 * KZ, curl_x, jnp.where(lane_r < 5 * KZ, curl_y, curl_z)),
+                    )
+                )
+            t.append(jnp.concatenate(modes, axis=0))
         high, low = split(jnp.concatenate(t, axis=1))
         rhs = jnp.concatenate([high, low, high, jnp.zeros((32, 256), bf16)], axis=0)
         o = dot(sy[...], rhs)
@@ -392,13 +415,13 @@
         out_specs=vmem,
         scratch_shapes=[
             *(pltpu.VMEM(t.shape, bf16) for t in consts[2:]),
-            pltpu.VMEM((2, 3, 24, 256), f32),
-            pltpu.VMEM((256, 256), f32),
+            pltpu.VMEM((3, 24, 256), f32),
+            pltpu.VMEM((128 * TILES, 256), f32),
             pltpu.VMEM((ORDERS, 3, XL, YL, N), f32),
             pltpu.VMEM((ORDERS, 3, XL, YL, N), f32),
             pltpu.VMEM((3, XL, YL, N), f32),
-            pltpu.VMEM((KY, N, 128), f32),
-            pltpu.VMEM((KY, N, 128), f32),
+            pltpu.VMEM((TILES, N, 128), f32),
+            pltpu.VMEM((TILES, N, 128), f32),
             pltpu.VMEM((XL, N, 128), f32),
             pltpu.VMEM((COLS, XL, YL, 128), f32),
             pltpu.VMEM((COLS, XL // 2, YL, 128), f32),

time: 72.5 us -> 69.4 us (0.957)
  Pallas kernels: 70.3 us -> 67.2 us
    pallas_call x1, Pallas kernels: 70.3 us -> 67.2 us  [shards(): pl.pallas_call(kernel, out_shape=jax.ShapeDtypeStruct((3, KY, KZ, MODES),...]
where the time goes in v2:
time: 69.4 us; the launch traced here: 69.3 us
  Pallas kernels  67.2 us (97%)
  other arithmetic  2.05 us (3%)
    pallas_call x1, Pallas kernels, shards(): pl.pallas_call(kernel, out_shape=jax.ShapeDtypeStruct((3, KY, KZ, MODES),...  67.2 us
    div x1, other arithmetic, shards(): return sums / (ORDERS + 1)  2.05 us

profile of v2, /device:TPU:1, one launch (start us, length us, event | category | flops | bytes accessed | tf_op | source)
XLA Modules:
  0.0 69.3 jit_solution(11609757541144260080)
XLA Ops:
  0.0 67.2 %euler_order.1 = f32[3,10,20,160]{3,2,1,0:T(8,128)} custom-call(f32[3,10,20,160]{3,2,1,0:T(8,128)} %a_ref.1, f32[6,3,16,32,256]{4,3,2,1,0:T(8,128)} %vel_hbm.1, f32[6,3,16,32,256]{4,3,2,1,0:T(8,128)} %vort_hbm.1, bf16[256,256]{1,0:T(8,128)(2,1)} %constant.23.clone.sxh, bf16[256,256]{1,0:T(8,128)(2,1)} %constant.24.clone.sxl, ...), custom_call_target="tpu_custom_call" | custom-call | tf_op jit(solution)/shard_map/euler_order/pallas_call | solution.py:411
  67.2 2.0 %broadcast_multiply_fusion = f32[3,10,20,160]{3,2,1,0:T(8,128)} fusion(f32[3,10,20,160]{3,2,1,0:T(8,128)} %euler_order.1), kind=kLoop, calls=%fused_computation | loop fusion | flops 96000 | bytes 768000 | tf_op jit(solution)/shard_map/div | solution.py:449

commit v3 on v2

--- a/solution.py
+++ b/solution.py
@@ -18,7 +18,7 @@
 XP = XC // 2
 OFFSETS = (0, 20, 40, 64, 84, 104)
 TILES = 8
-TABLES = 8
+TABLES = 10
 MESH = pl.DeviceIdType.MESH
 bf16, f32 = jnp.bfloat16, jnp.float32
 
@@ -42,7 +42,7 @@
 def tables():
     s = basis()
     sx = np.zeros((N, 256))
-    sx[:, :MODES] = s
+    sx[:, :MODES] = s.reshape(ROWS, 2, 8, MODES).transpose(1, 0, 2, 3).reshape(N, MODES)
     order = np.arange(MODES).reshape(ROWS, KY).T.reshape(-1)
     sy_h, sy_l = halves(s[:, order])
     sy = np.concatenate([sy_h, sy_h, sy_l, np.zeros((N, 32), jnp.bfloat16)], axis=1)
@@ -87,13 +87,13 @@
 
 
 def kernel(
-    a_ref, vel_hbm, vort_hbm, sxh, sxl, *rest,
+    a_hbm, vel_hbm, vort_hbm, *rest,
 ):
     tables_hbm, (out_ref, *tables_vmem), rest = rest[:TABLES], rest[TABLES : 2 * TABLES + 1], rest[2 * TABLES + 1 :]
-    sy, szh, szl, zah, zal, ya, xah, xal = tables_vmem
+    sxh, sxl, sy, szh, szl, zah, zal, ya, xah, xal = tables_vmem
     (
-    a_s, f_s, vel, vort, part, send1, recv1, send2, recv2, send3, recv3, send4, recv4, fin,
-    hbm_sem, table_sem, s1s, s1r, s2s, s2r, s3s, s3r, s4s, s4r, own,
+    a_ref, a_s, f_s, vel, vort, part, send1, recv1, send2, recv2, send3, recv3, send4, recv4, fin,
+    hbm_sem, a_sem, table_sem, s1s, s1r, s2s, s2r, s3s, s3r, s4s, s4r, own,
     ) = rest
     r, c = lax.axis_index("row"), lax.axis_index("col")
 
@@ -118,11 +118,10 @@
     def table(i):
         return pltpu.make_async_copy(tables_hbm[i], tables_vmem[i], table_sem.at[i])
 
-    for i in range(TABLES):
-        table(i).start()
-    for o in (1, 5, 2, 4, 3, 0):
-        for copy in stored(o):
-            copy.start()
+    first = pltpu.make_async_copy(a_hbm, a_ref, a_sem)
+    first.start()
+    table(0).start()
+    table(1).start()
 
     def ds(start, size, unit):
         return pl.ds(pl.multiple_of(start, unit), size)
@@ -130,8 +129,8 @@
     def copy1(h, i):
         there = row_peer(i)
         return pltpu.make_async_remote_copy(
-            send1.at[:, ds(there * XL + 8 * h, 8, 8), :],
-            recv1.at[:, ds(r * XL + 8 * h, 8, 8), :],
+            send1.at[:, h, ds(there * 8, 8, 8), :],
+            recv1.at[:, h, ds(r * 8, 8, 8), :],
             s1s.at[h, i], s1r.at[h, i], device_id=(there, c), device_id_type=MESH,
         )
 
@@ -159,21 +158,24 @@
             s4s.at[h, i], s4r.at[h, i], device_id=(there, c), device_id_type=MESH,
         )
 
-    own1 = pltpu.make_async_copy(send1.at[:, ds(r * XL, XL, 8), :], recv1.at[:, ds(r * XL, XL, 8), :], own.at[0])
+    def own1(h):
+        return pltpu.make_async_copy(
+            send1.at[:, h, ds(r * 8, 8, 8), :], recv1.at[:, h, ds(r * 8, 8, 8), :], own.at[h]
+        )
 
     def own4(h):
         return pltpu.make_async_copy(
-            send4.at[h, :, ds(r * 8, 8, 8), :], recv4.at[h, :, ds(r * 8, 8, 8), :], own.at[1 + h]
+            send4.at[h, :, ds(r * 8, 8, 8), :], recv4.at[h, :, ds(r * 8, 8, 8), :], own.at[2 + h]
         )
 
     def own2(g):
         return pltpu.make_async_copy(
-            send2.at[pl.ds(g * XC, XC), ds(c * YL, YL, 8), :], recv2.at[c, pl.ds(g * XC, XC)], own.at[3 + g]
+            send2.at[pl.ds(g * XC, XC), ds(c * YL, YL, 8), :], recv2.at[c, pl.ds(g * XC, XC)], own.at[4 + g]
         )
 
     def own3(g):
         return pltpu.make_async_copy(
-            send3.at[c, pl.ds(g * XP, XP)], recv3.at[pl.ds(g * XP, XP), ds(c * YL, YL, 8), :], own.at[3 + CHUNKS + g]
+            send3.at[c, pl.ds(g * XP, XP)], recv3.at[pl.ds(g * XP, XP), ds(c * YL, YL, 8), :], own.at[4 + CHUNKS + g]
         )
 
     lane = lax.broadcasted_iota(jnp.int32, (24, 256), 1)
@@ -192,6 +194,7 @@
 
     a_s[...] = jnp.zeros_like(a_s)
     f_s[...] = jnp.zeros_like(f_s)
+    first.wait()
     for m in range(KY):
         for i in range(3):
             a_s[i, 0:KZ, 0:MODES] = a_ref[i, m]
@@ -201,19 +204,27 @@
             first = KZ * (5 * m + i)
             f_s[first : first + KZ, :] = v[i][0:KZ]
 
-    for t in range(TILES // 2):
-        high, low = split(f_s[256 * t : 256 * t + 256, :])
-        o = dot_nt(sxh[...], high) + (dot_nt(sxh[...], low) + dot_nt(sxl[...], high))
-        send1[2 * t] = o[:, :128]
-        send1[2 * t + 1] = o[:, 128:]
-
-    own1.start()
-    pl.semaphore_wait(barrier, ROWS + COLS - 2)
+    table(0).wait()
+    table(1).wait()
+    for i in range(2, TABLES):
+        table(i).start()
+    for o in (1, 5, 2, 4, 3, 0):
+        for copy in stored(o):
+            copy.start()
     for h in range(2):
+        part_h, part_l = sxh[128 * h : 128 * h + 128, :], sxl[128 * h : 128 * h + 128, :]
+        for t in range(TILES // 2):
+            high, low = split(f_s[256 * t : 256 * t + 256, :])
+            o = dot_nt(part_h, high) + (dot_nt(part_h, low) + dot_nt(part_l, high))
+            send1[2 * t, h] = o[:, :128]
+            send1[2 * t + 1, h] = o[:, 128:]
+        own1(h).start()
+        if h == 0:
+            pl.semaphore_wait(barrier, ROWS + COLS - 2)
         for i in range(1, ROWS):
             copy1(h, i).start()
 
-    for i in range(TABLES):
+    for i in range(2, TABLES):
         table(i).wait()
     for o in (1, 5, 2, 4, 3):
         for copy in stored(o):
@@ -238,11 +249,11 @@
     sub_r = lax.broadcasted_iota(jnp.int32, (ROWS, 128), 0)
     slope_z = (lane_r % KZ // 2 + c * (KZ // 2)).astype(f32) / KMAX
 
-    def synth_y(xp, carry):
+    def synth_y(h, xp):
         t = []
         for k in range(2):
-            rows = pl.ds(2 * xp + k, ROWS, stride=XL)
-            tiles = [recv1[m, rows, :] for m in range(TILES)]
+            rows = pl.ds(2 * xp + k - 8 * h, ROWS, stride=8)
+            tiles = [recv1[m, h, rows, :] for m in range(TILES)]
             sent = []
             for m in range(KY):
                 tile, first = divmod(5 * KZ * m, 128)
@@ -272,14 +283,13 @@
         o = dot(sy[...], rhs)
         send2[2 * xp] = o[:, :128]
         send2[2 * xp + 1] = o[:, 128:]
-        return carry
-
-    own1.wait()
+
     for h in range(2):
+        own1(h).wait()
         for i in range(1, ROWS):
             copy1(h, i).wait_recv()
         for g in range(h * CHUNKS // 2, (h + 1) * CHUNKS // 2):
-            lax.fori_loop(g * XP, (g + 1) * XP, synth_y, 0)
+            lax.fori_loop(g * XP, (g + 1) * XP, lambda xp, carry: (synth_y(h, xp), carry)[1], 0)
             own2(g).start()
             for i in range(1, COLS):
                 copy2(g, i).start()
@@ -406,22 +416,23 @@
 def shards(new_velocity, stored_velocity, stored_vorticity):
     consts = tables()
     vmem = pl.BlockSpec(memory_space=pltpu.VMEM)
-    hbm = pl.BlockSpec(memory_space=pl.ANY)
+    hbm = pl.BlockSpec(memory_space=pltpu.HBM)
     dma = pltpu.SemaphoreType.DMA
     sums = pl.pallas_call(
         kernel,
         out_shape=jax.ShapeDtypeStruct((3, KY, KZ, MODES), f32),
-        in_specs=[vmem, hbm, hbm, vmem, vmem] + [hbm] * TABLES,
+        in_specs=[hbm, hbm, hbm] + [hbm] * TABLES,
         out_specs=vmem,
         scratch_shapes=[
-            *(pltpu.VMEM(t.shape, bf16) for t in consts[2:]),
+            *(pltpu.VMEM(t.shape, bf16) for t in consts),
+            pltpu.VMEM((3, KY, KZ, MODES), f32),
             pltpu.VMEM((3, 24, 256), f32),
             pltpu.VMEM((128 * TILES, 256), f32),
             pltpu.VMEM((ORDERS, 3, XL, YL, N), f32),
             pltpu.VMEM((ORDERS, 3, XL, YL, N), f32),
             pltpu.VMEM((3, XL, YL, N), f32),
-            pltpu.VMEM((TILES, N, 128), f32),
-            pltpu.VMEM((TILES, N, 128), f32),
+            pltpu.VMEM((TILES, 2, 128, 128), f32),
+            pltpu.VMEM((TILES, 2, 128, 128), f32),
             pltpu.VMEM((XL, N, 128), f32),
             pltpu.VMEM((COLS, XL, YL, 128), f32),
             pltpu.VMEM((COLS, XL // 2, YL, 128), f32),
@@ -430,6 +441,7 @@
             pltpu.VMEM((2, KY // 2, 128, 128), f32),
             pltpu.VMEM((KY // 2 * 64, 512), f32),
             dma((2, ORDERS)),
+            dma,
             dma((TABLES,)),
             dma((2, ROWS)),
             dma((2, ROWS)),
@@ -439,13 +451,13 @@
             dma((CHUNKS, COLS)),
             dma((2, ROWS)),
             dma((2, ROWS)),
-            dma((3 + 2 * CHUNKS,)),
+            dma((4 + 2 * CHUNKS,)),
         ],
         compiler_params=pltpu.CompilerParams(
-            collective_id=0, has_side_effects=True, vmem_limit_bytes=60 * 2**20
+            collective_id=0, has_side_effects=True, vmem_limit_bytes=46 * 2**20
         ),
         name="euler_order",
-    )(new_velocity, stored_velocity, stored_vorticity, *map(jnp.asarray, consts))
+    )(*(pltpu.with_memory_space_constraint(x, pltpu.HBM) for x in (new_velocity, stored_velocity, stored_vorticity, *map(jnp.asarray, consts))))
     return sums / (ORDERS + 1)
 
 

time: 69.4 us -> 66.5 us (0.958)
  Pallas kernels: 67.2 us -> 65.4 us
  other arithmetic: 2.05 us -> 0.94 us
    pallas_call x1, Pallas kernels: 67.2 us -> 65.4 us  [shards(): pl.pallas_call(kernel, out_shape=jax.ShapeDtypeStruct((3, KY, KZ, MODES),...]
    div x1, other arithmetic: 2.05 us -> 0.94 us  [shards(): return sums / (ORDERS + 1)]
where the time goes in v3:
time: 66.5 us; the launch traced here: 66.4 us
  Pallas kernels  65.4 us (98%)
  other arithmetic  0.94 us (1%)
    pallas_call x1, Pallas kernels, shards(): pl.pallas_call(kernel, out_shape=jax.ShapeDtypeStruct((3, KY, KZ, MODES),...  65.4 us

profile of v3, /device:TPU:1, one launch (start us, length us, event | category | flops | bytes accessed | tf_op | source)
XLA Modules:
  0.0 66.4 jit_solution(12232134110871128097)
XLA Ops:
  0.0 65.4 %euler_order.1 = f32[3,10,20,160]{3,2,1,0:T(8,128)S(1)} custom-call(f32[3,10,20,160]{3,2,1,0:T(8,128)} %a_hbm.1, f32[6,3,16,32,256]{4,3,2,1,0:T(8,128)} %vel_hbm.1, f32[6,3,16,32,256]{4,3,2,1,0:T(8,128)} %vort_hbm.1, bf16[256,256]{1,0:T(8,128)(2,1)} %constant.23.clone.rest_0_, bf16[256,256]{1,0:T(8,128)(2,1)} %constant.24.clone.rest_1_, ...), custom_call_target="tpu_custom_call" | custom-call | tf_op jit(solution)/shard_map/euler_order/pallas_call | solution.py:421
  65.4 0.9 %broadcast_multiply_fusion = f32[3,10,20,160]{3,2,1,0:T(8,128)} fusion(f32[3,10,20,160]{3,2,1,0:T(8,128)S(1)} %euler_order.1), kind=kLoop, calls=%fused_computation | loop fusion | flops 96000 | bytes 768000 | tf_op jit(solution)/shard_map/div | solution.py:461

commit v4 on v3

--- a/solution.py
+++ b/solution.py
@@ -18,6 +18,7 @@
 XP = XC // 2
 OFFSETS = (0, 20, 40, 64, 84, 104)
 TILES = 8
+BLOCK1, BLOCK4 = 8 * TILES, 8 * (KY // 2)
 TABLES = 10
 MESH = pl.DeviceIdType.MESH
 bf16, f32 = jnp.bfloat16, jnp.float32
@@ -103,35 +104,35 @@
     def col_peer(i):
         return lax.rem(c + i, COLS)
 
+    def stored(o):
+        return (
+            pltpu.make_async_copy(vel_hbm.at[o], vel.at[o], hbm_sem.at[0, o]),
+            pltpu.make_async_copy(vort_hbm.at[o], vort.at[o], hbm_sem.at[1, o]),
+        )
+
+    def table(i):
+        return pltpu.make_async_copy(tables_hbm[i], tables_vmem[i], table_sem.at[i])
+
+    first = pltpu.make_async_copy(a_hbm, a_ref, a_sem)
+    first.start()
+    table(0).start()
+    table(1).start()
+
     barrier = pltpu.get_barrier_semaphore()
     for i in range(1, ROWS):
         pl.semaphore_signal(barrier, 1, device_id=(row_peer(i), c), device_id_type=MESH)
     for i in range(1, COLS):
         pl.semaphore_signal(barrier, 1, device_id=(r, col_peer(i)), device_id_type=MESH)
 
-    def stored(o):
-        return (
-            pltpu.make_async_copy(vel_hbm.at[o], vel.at[o], hbm_sem.at[0, o]),
-            pltpu.make_async_copy(vort_hbm.at[o], vort.at[o], hbm_sem.at[1, o]),
-        )
-
-    def table(i):
-        return pltpu.make_async_copy(tables_hbm[i], tables_vmem[i], table_sem.at[i])
-
-    first = pltpu.make_async_copy(a_hbm, a_ref, a_sem)
-    first.start()
-    table(0).start()
-    table(1).start()
-
     def ds(start, size, unit):
         return pl.ds(pl.multiple_of(start, unit), size)
 
     def copy1(h, i):
         there = row_peer(i)
         return pltpu.make_async_remote_copy(
-            send1.at[:, h, ds(there * 8, 8, 8), :],
-            recv1.at[:, h, ds(r * 8, 8, 8), :],
-            s1s.at[h, i], s1r.at[h, i], device_id=(there, c), device_id_type=MESH,
+            send1.at[h, ds(there * BLOCK1, BLOCK1, 8), :],
+            recv1.at[h, ds(r * BLOCK1, BLOCK1, 8), :],
+            s1s.at[h], s1r.at[h], device_id=(there, c), device_id_type=MESH,
         )
 
     def copy2(g, i):
@@ -139,7 +140,7 @@
         return pltpu.make_async_remote_copy(
             send2.at[pl.ds(g * XC, XC), ds(there * YL, YL, 8), :],
             recv2.at[c, pl.ds(g * XC, XC)],
-            s2s.at[g, i], s2r.at[g, i], device_id=(r, there), device_id_type=MESH,
+            s2s.at[g], s2r.at[g], device_id=(r, there), device_id_type=MESH,
         )
 
     def copy3(g, i):
@@ -147,25 +148,50 @@
         return pltpu.make_async_remote_copy(
             send3.at[there, pl.ds(g * XP, XP)],
             recv3.at[pl.ds(g * XP, XP), ds(c * YL, YL, 8), :],
-            s3s.at[g, i], s3r.at[g, i], device_id=(r, there), device_id_type=MESH,
+            s3s.at[g], s3r.at[g], device_id=(r, there), device_id_type=MESH,
         )
 
     def copy4(h, i):
         there = row_peer(i)
         return pltpu.make_async_remote_copy(
-            send4.at[h, :, ds(there * 8, 8, 8), :],
-            recv4.at[h, :, ds(r * 8, 8, 8), :],
-            s4s.at[h, i], s4r.at[h, i], device_id=(there, c), device_id_type=MESH,
-        )
+            send4.at[h, ds(there * BLOCK4, BLOCK4, 8), :],
+            recv4.at[h, ds(r * BLOCK4, BLOCK4, 8), :],
+            s4s.at[h], s4r.at[h], device_id=(there, c), device_id_type=MESH,
+        )
+
+    def all_of(source, target, sent, arrived):
+        return pltpu.make_async_remote_copy(
+            source, target, sent, arrived, device_id=(row_peer(1), c), device_id_type=MESH
+        )
+
+    def all1(h):
+        rows = pl.ds(0, (ROWS - 1) * BLOCK1)
+        return all_of(send1.at[h, rows], recv1.at[h, rows], s1s.at[h], s1r.at[h])
+
+    def all2(g):
+        piece = pl.ds(g * XC, XC)
+        return all_of(
+            send2.at[piece, pl.ds(0, (COLS - 1) * YL)], recv2.at[pl.ds(0, COLS - 1), piece], s2s.at[g], s2r.at[g]
+        )
+
+    def all3(g):
+        piece = pl.ds(g * XP, XP)
+        return all_of(
+            send3.at[pl.ds(0, COLS - 1), piece], recv3.at[piece, pl.ds(0, (COLS - 1) * YL)], s3s.at[g], s3r.at[g]
+        )
+
+    def all4(h):
+        rows = pl.ds(0, (ROWS - 1) * BLOCK4)
+        return all_of(send4.at[h, rows], recv4.at[h, rows], s4s.at[h], s4r.at[h])
 
     def own1(h):
         return pltpu.make_async_copy(
-            send1.at[:, h, ds(r * 8, 8, 8), :], recv1.at[:, h, ds(r * 8, 8, 8), :], own.at[h]
+            send1.at[h, ds(r * BLOCK1, BLOCK1, 8), :], recv1.at[h, ds(r * BLOCK1, BLOCK1, 8), :], own.at[h]
         )
 
     def own4(h):
         return pltpu.make_async_copy(
-            send4.at[h, :, ds(r * 8, 8, 8), :], recv4.at[h, :, ds(r * 8, 8, 8), :], own.at[2 + h]
+            send4.at[h, ds(r * BLOCK4, BLOCK4, 8), :], recv4.at[h, ds(r * BLOCK4, BLOCK4, 8), :], own.at[2 + h]
         )
 
     def own2(g):
@@ -216,8 +242,10 @@
         for t in range(TILES // 2):
             high, low = split(f_s[256 * t : 256 * t + 256, :])
             o = dot_nt(part_h, high) + (dot_nt(part_h, low) + dot_nt(part_l, high))
-            send1[2 * t, h] = o[:, :128]
-            send1[2 * t + 1, h] = o[:, 128:]
+            for k in range(2):
+                for there in range(ROWS):
+                    first_row = BLOCK1 * there + 8 * (2 * t + k)
+                    send1[h, first_row : first_row + 8, :] = o[8 * there : 8 * there + 8, 128 * k : 128 * k + 128]
         own1(h).start()
         if h == 0:
             pl.semaphore_wait(barrier, ROWS + COLS - 2)
@@ -252,8 +280,7 @@
     def synth_y(h, xp):
         t = []
         for k in range(2):
-            rows = pl.ds(2 * xp + k - 8 * h, ROWS, stride=8)
-            tiles = [recv1[m, h, rows, :] for m in range(TILES)]
+            tiles = [recv1[h, pl.ds(8 * m + 2 * xp + k - 8 * h, ROWS, stride=BLOCK1), :] for m in range(TILES)]
             sent = []
             for m in range(KY):
                 tile, first = divmod(5 * KZ * m, 128)
@@ -286,8 +313,7 @@
 
     for h in range(2):
         own1(h).wait()
-        for i in range(1, ROWS):
-            copy1(h, i).wait_recv()
+        all1(h).wait_recv()
         for g in range(h * CHUNKS // 2, (h + 1) * CHUNKS // 2):
             lax.fori_loop(g * XP, (g + 1) * XP, lambda xp, carry: (synth_y(h, xp), carry)[1], 0)
             own2(g).start()
@@ -336,8 +362,7 @@
 
     for g in range(CHUNKS):
         own2(g).wait()
-        for i in range(1, COLS):
-            copy2(g, i).wait_recv()
+        all2(g).wait_recv()
         lax.fori_loop(g * XP, (g + 1) * XP, middle, 0)
         own3(g).start()
         for i in range(1, COLS):
@@ -348,13 +373,14 @@
         o = dot(ya[...], jnp.concatenate([high, low, high], axis=0))
         for k in range(2):
             for m in range(KY):
-                rows = pl.ds(4 * (m % 2) + 2 * xq - 4 * h + k, ROWS, stride=8)
-                send4[h, m // 2, rows, :] = o[ROWS * m : ROWS * (m + 1), 128 * k : 128 * k + 128]
+                rows = pl.ds(8 * (m // 2) + 4 * (m % 2) + 2 * xq - 4 * h + k, ROWS, stride=BLOCK4)
+                send4[h, rows, :] = o[ROWS * m : ROWS * (m + 1), 128 * k : 128 * k + 128]
 
     def analyze_x(h):
         rows = []
         for m in range(KY // 2):
-            t = recv4[h, m].T
+            firsts = [BLOCK4 * there + 8 * m for there in range(ROWS)]
+            t = jnp.concatenate([recv4[h, first_row : first_row + 8, :] for first_row in firsts], axis=0).T
             rows.append(jnp.concatenate([t[0:64], t[64:128]], axis=1))
         high, low = split(jnp.concatenate(rows, axis=0))
         part_h, part_l = xah[256 * h : 256 * h + 256, :], xal[256 * h : 256 * h + 256, :]
@@ -363,17 +389,21 @@
     for h in range(2):
         for g in range(h * CHUNKS // 2, (h + 1) * CHUNKS // 2):
             own3(g).wait()
-            for i in range(1, COLS):
-                copy3(g, i).wait_recv()
+            all3(g).wait_recv()
             for q in range(g * XP // 2, (g + 1) * XP // 2):
                 analyze_y(h, q)
         own4(h).start()
         for i in range(1, ROWS):
             copy4(h, i).start()
     for h in range(2):
+        all1(h).wait_send()
+    for g in range(CHUNKS):
+        all2(g).wait_send()
+        all3(g).wait_send()
+    for h in range(2):
         own4(h).wait()
-        for i in range(1, ROWS):
-            copy4(h, i).wait_recv()
+        all4(h).wait_send()
+        all4(h).wait_recv()
         if h == 0:
             fin[...] = analyze_x(0)
         else:
@@ -403,15 +433,6 @@
     for pair in range(KY // 2):
         finish(pair, 0)
 
-    for h in range(2):
-        for i in range(1, ROWS):
-            copy1(h, i).wait_send()
-            copy4(h, i).wait_send()
-    for g in range(CHUNKS):
-        for i in range(1, COLS):
-            copy2(g, i).wait_send()
-            copy3(g, i).wait_send()
-
 
 def shards(new_velocity, stored_velocity, stored_vorticity):
     consts = tables()
@@ -431,26 +452,26 @@
             pltpu.VMEM((ORDERS, 3, XL, YL, N), f32),
             pltpu.VMEM((ORDERS, 3, XL, YL, N), f32),
             pltpu.VMEM((3, XL, YL, N), f32),
-            pltpu.VMEM((TILES, 2, 128, 128), f32),
-            pltpu.VMEM((TILES, 2, 128, 128), f32),
+            pltpu.VMEM((2, ROWS * BLOCK1, 128), f32),
+            pltpu.VMEM((2, ROWS * BLOCK1, 128), f32),
             pltpu.VMEM((XL, N, 128), f32),
             pltpu.VMEM((COLS, XL, YL, 128), f32),
             pltpu.VMEM((COLS, XL // 2, YL, 128), f32),
             pltpu.VMEM((XL // 2, N, 128), f32),
-            pltpu.VMEM((2, KY // 2, 128, 128), f32),
-            pltpu.VMEM((2, KY // 2, 128, 128), f32),
+            pltpu.VMEM((2, ROWS * BLOCK4, 128), f32),
+            pltpu.VMEM((2, ROWS * BLOCK4, 128), f32),
             pltpu.VMEM((KY // 2 * 64, 512), f32),
             dma((2, ORDERS)),
             dma,
             dma((TABLES,)),
-            dma((2, ROWS)),
-            dma((2, ROWS)),
-            dma((CHUNKS, COLS)),
-            dma((CHUNKS, COLS)),
-            dma((CHUNKS, COLS)),
-            dma((CHUNKS, COLS)),
-            dma((2, ROWS)),
-            dma((2, ROWS)),
+            dma((2,)),
+            dma((2,)),
+            dma((CHUNKS,)),
+            dma((CHUNKS,)),
+            dma((CHUNKS,)),
+            dma((CHUNKS,)),
+            dma((2,)),
+            dma((2,)),
             dma((4 + 2 * CHUNKS,)),
         ],
         compiler_params=pltpu.CompilerParams(

time: 66.5 us -> 64.2 us (0.965)
  Pallas kernels: 65.4 us -> 63.1 us
    pallas_call x1, Pallas kernels: 65.4 us -> 63.1 us  [shards(): pl.pallas_call(kernel, out_shape=jax.ShapeDtypeStruct((3, KY, KZ, MODES),...]
where the time goes in v4:
time: 64.2 us; the launch traced here: 64.1 us
  Pallas kernels  63.1 us (98%)
  other arithmetic  0.94 us (1%)
    pallas_call x1, Pallas kernels, shards(): pl.pallas_call(kernel, out_shape=jax.ShapeDtypeStruct((3, KY, KZ, MODES),...  63.1 us

profile of v4, /device:TPU:1, one launch (start us, length us, event | category | flops | bytes accessed | tf_op | source)
XLA Modules:
  0.0 64.1 jit_solution(7052109568838663179)
XLA Ops:
  0.0 63.1 %euler_order.1 = f32[3,10,20,160]{3,2,1,0:T(8,128)S(1)} custom-call(f32[3,10,20,160]{3,2,1,0:T(8,128)} %a_hbm.1, f32[6,3,16,32,256]{4,3,2,1,0:T(8,128)} %vel_hbm.1, f32[6,3,16,32,256]{4,3,2,1,0:T(8,128)} %vort_hbm.1, bf16[256,256]{1,0:T(8,128)(2,1)} %constant.23.clone.rest_0_, bf16[256,256]{1,0:T(8,128)(2,1)} %constant.24.clone.rest_1_, ...), custom_call_target="tpu_custom_call" | custom-call | tf_op jit(solution)/shard_map/euler_order/pallas_call | solution.py:442
  63.1 0.9 %broadcast_multiply_fusion = f32[3,10,20,160]{3,2,1,0:T(8,128)} fusion(f32[3,10,20,160]{3,2,1,0:T(8,128)S(1)} %euler_order.1), kind=kLoop, calls=%fused_computation | loop fusion | flops 96000 | bytes 768000 | tf_op jit(solution)/shard_map/div | solution.py:482

commit v5 on v4

--- a/solution.py
+++ b/solution.py
@@ -219,7 +219,7 @@
         return wave_z * pair_swap(v, 0)
 
     a_s[...] = jnp.zeros_like(a_s)
-    f_s[...] = jnp.zeros_like(f_s)
+    f_s[5 * KY * KZ :, :] = jnp.zeros((128 * TILES - 5 * KY * KZ, 256), f32)
     first.wait()
     for m in range(KY):
         for i in range(3):
@@ -316,9 +316,9 @@
         all1(h).wait_recv()
         for g in range(h * CHUNKS // 2, (h + 1) * CHUNKS // 2):
             lax.fori_loop(g * XP, (g + 1) * XP, lambda xp, carry: (synth_y(h, xp), carry)[1], 0)
-            own2(g).start()
             for i in range(1, COLS):
                 copy2(g, i).start()
+            own2(g).start()
 
     lane_y = lax.broadcasted_iota(jnp.int32, (YL, 128), 1)
 
@@ -364,9 +364,9 @@
         own2(g).wait()
         all2(g).wait_recv()
         lax.fori_loop(g * XP, (g + 1) * XP, middle, 0)
-        own3(g).start()
         for i in range(1, COLS):
             copy3(g, i).start()
+        own3(g).start()
 
     def analyze_y(h, xq):
         high, low = split(jnp.concatenate([recv3[2 * xq], recv3[2 * xq + 1]], axis=1))
@@ -392,9 +392,9 @@
             all3(g).wait_recv()
             for q in range(g * XP // 2, (g + 1) * XP // 2):
                 analyze_y(h, q)
-        own4(h).start()
         for i in range(1, ROWS):
             copy4(h, i).start()
+        own4(h).start()
     for h in range(2):
         all1(h).wait_send()
     for g in range(CHUNKS):

time: 64.2 us -> 64.1 us (level)
  no operation moved by 1% of the time
where the time goes in v5:
time: 64.1 us; the launch traced here: 63.9 us
  Pallas kernels  63 us (98%)
  other arithmetic  0.94 us (1%)
    pallas_call x1, Pallas kernels, shards(): pl.pallas_call(kernel, out_shape=jax.ShapeDtypeStruct((3, KY, KZ, MODES),...  63 us

profile of v5, /device:TPU:1, one launch (start us, length us, event | category | flops | bytes accessed | tf_op | source)
XLA Modules:
  0.0 63.9 jit_solution(3511268542883459014)
XLA Ops:
  0.0 63.0 %euler_order.1 = f32[3,10,20,160]{3,2,1,0:T(8,128)S(1)} custom-call(f32[3,10,20,160]{3,2,1,0:T(8,128)} %a_hbm.1, f32[6,3,16,32,256]{4,3,2,1,0:T(8,128)} %vel_hbm.1, f32[6,3,16,32,256]{4,3,2,1,0:T(8,128)} %vort_hbm.1, bf16[256,256]{1,0:T(8,128)(2,1)} %constant.23.clone.rest_0_, bf16[256,256]{1,0:T(8,128)(2,1)} %constant.24.clone.rest_1_, ...), custom_call_target="tpu_custom_call" | custom-call | tf_op jit(solution)/shard_map/euler_order/pallas_call | solution.py:442
  63.0 0.9 %broadcast_multiply_fusion = f32[3,10,20,160]{3,2,1,0:T(8,128)} fusion(f32[3,10,20,160]{3,2,1,0:T(8,128)S(1)} %euler_order.1), kind=kLoop, calls=%fused_computation | loop fusion | flops 96000 | bytes 768000 | tf_op jit(solution)/shard_map/div | solution.py:482
